TPU v7x, 512 devices: a whole 4x4x16 slice. The times are simulated.
512 devices in a mesh: head: 8 (over x, core), shard: 64 (over y, z).
Axes of the slice: x: 4, y: 4, z: 16, core: 2. Of those that a mesh axis runs over, the one named last changes fastest.
Arguments:
- tokens: bfloat16 [256, 64, 1024], P('shard'), may hold values from -6 to 6
- w_query: bfloat16 [1024, 1024], P(None, 'head'), may hold values from -0.1875 to 0.1875
- w_key: bfloat16 [1024, 1024], P(None, 'head'), may hold values from -0.1875 to 0.1875
- w_value: bfloat16 [1024, 1024], P(None, 'head'), may hold values from -0.1875 to 0.1875
- w_out: bfloat16 [1024, 1024], P('head'), may hold values from -0.1875 to 0.1875
- norm1_gain: float32 [1024], replicated, may hold values from 0.1 to 1.9
- w_inner: bfloat16 [1024, 4096], P(None, 'head'), may hold values from -0.1875 to 0.1875
- w_outer: bfloat16 [4096, 1024], P('head'), may hold values from -0.09375 to 0.09375
- norm2_gain: float32 [1024], replicated, may hold values from 0.1 to 1.9
- w_project: bfloat16 [1024, 128], replicated, may hold values from -0.1875 to 0.1875
- key_pages: bfloat16 [128, 64, 1024], P('shard', None, 'head'), may hold values from -400 to 400
- value_pages: bfloat16 [128, 64, 1024], P('shard', None, 'head'), may hold values from -6 to 6
- page_table: int32 [128], replicated, may hold values from 0 to 127, as said below
- prompt_lengths: int32 [16], replicated, may hold values from 1 to 512
- request_group: int32 [256], P('shard'), may hold values from 0 to 15, as said below
- doc_vectors: bfloat16 [131072, 128], P(('head', 'shard')), may hold values from -0.29882812 to 0.29882812
- doc_lengths: int32 [512, 4], P(('head', 'shard')), may hold values from 1 to 128, 256 in all within a row
- candidates: int32 [256, 16], P('shard'), may hold values from 0 to 2047, as said below
Outputs:
- embedded: bfloat16 [256, 64, 128], P('shard')
- scores: float32 [256, 16], P('shard')
Inputs may be any that keep to these rules, and one draw needn't show every extreme that they name: `page_table`: positions g * 8 to g * 8 + 7 list the pages of group g's prompt in order; they are the pages g * 8 to g * 8 + 7 in some order. `request_group`: every group has exactly 16 requests; the 4 requests of one index of shard belong to distinct groups. `candidates`: document d is held by the device of index d // 4 along head+shard. `doc_lengths`: each row holds the token counts of one holder's documents in the order they are packed; a row sums to 256.
All inputs are finite; a program needn't handle non-finite values.
Results may differ from a plain program's by a relative error of at most 0.023.
Values may be sent and summed in bfloat16 or wider, within the bound.
No kernel may reach another device: no remote copies, remote signals or barrier semaphores. Data moves between devices by JAX's collectives and lax.ppermute only.
A program may use at most 64 MiB of HBM per device.

v0:
```python
import math
import jax
import jax.numpy as jnp
from jax import lax
from jax.sharding import PartitionSpec as P

DH = 64
PPG = 8
DLMAX = 128


def layer_norm(values, norm_gain):
    row_mean = jnp.mean(values, axis=-1, keepdims=True)
    row_var = jnp.mean(jnp.square(values - row_mean), axis=-1, keepdims=True)
    return (values - row_mean) * lax.rsqrt(row_var + 1e-05) * norm_gain


def combine_heads(term_rows, residual, norm_gain):
    row_total = residual.shape[0]
    summed = lax.psum(term_rows(0, row_total).astype(jnp.bfloat16), "head").astype(jnp.float32)
    return layer_norm(residual.astype(jnp.float32) + summed, norm_gain).astype(jnp.bfloat16)


def build_tiles(vectors, lengths):
    holders = lengths.shape[0]
    per_holder = vectors.shape[0] // holders
    starts = (
        jnp.arange(holders, dtype=jnp.int32)[:, None] * per_holder
        + jnp.cumsum(lengths, axis=1)
        - lengths
    )
    tile_index = starts.reshape(-1)[:, None] + jnp.arange(DLMAX, dtype=jnp.int32)[None, :]
    tile_valid = jnp.arange(DLMAX)[None, :] < lengths.reshape(-1)[:, None]
    tile_index = jnp.minimum(tile_index, vectors.shape[0] - 1)
    doc_tiles = jnp.take(vectors, tile_index.reshape(-1), axis=0)
    return (doc_tiles, tile_valid)


def doc_maxima(query_rows, doc_tiles, tile_valid):
    row_count = query_rows.shape[0]
    row_block = math.gcd(row_count, 256)
    docs_here = tile_valid.shape[0]

    def block_max(block_rows):
        sims = jnp.einsum("ne,te->nt", block_rows, doc_tiles, preferred_element_type=jnp.float32)
        sims = sims.reshape(row_block, docs_here, DLMAX)
        return jnp.max(jnp.where(tile_valid[None], sims, -1e30), axis=-1)

    blocks = query_rows.reshape(row_count // row_block, row_block, query_rows.shape[1])
    return lax.map(block_max, blocks).reshape(row_count, docs_here)


def per_device(
    tokens,
    w_query,
    w_key,
    w_value,
    w_out,
    norm1_gain,
    w_inner,
    w_outer,
    norm2_gain,
    w_project,
    key_pages,
    value_pages,
    page_table,
    prompt_lengths,
    request_group,
    doc_vectors,
    doc_lengths,
    candidates,
):
    req_count, query_len, model_width = tokens.shape
    head_width = w_query.shape[1]
    heads_here = head_width // DH
    token_rows = tokens.reshape(req_count * query_len, model_width)

    def project(weight):
        out = jnp.dot(token_rows, weight, preferred_element_type=jnp.float32).astype(jnp.bfloat16)
        return out.reshape(req_count, query_len, heads_here, DH)

    queries = project(w_query)
    keys_own = project(w_key)
    values_own = project(w_value)
    score_scale = 1.0 / math.sqrt(DH)
    own_score = (
        jnp.einsum("rqhd,rkhd->rhqk", queries, keys_own, preferred_element_type=jnp.float32)
        * score_scale
    )
    row_top = jnp.max(own_score, axis=-1)
    own_weight = jnp.exp(own_score - row_top[..., None])
    row_total = jnp.sum(own_weight, axis=-1)
    weighted = jnp.einsum(
        "rhqk,rkhd->rhqd",
        own_weight.astype(jnp.bfloat16),
        values_own,
        preferred_element_type=jnp.float32,
    )
    cand_ids = lax.all_gather(candidates, "shard", axis=0, tiled=True)
    group_count = prompt_lengths.shape[0]
    page_slot = jnp.argsort(page_table)
    group_hit = request_group[:, None] == jnp.arange(group_count, dtype=jnp.int32)[None, :]
    group_len = jnp.sum(jnp.where(group_hit, prompt_lengths[None, :], 0), axis=1)
    running = (row_top, row_total, weighted)
    key_piece = lax.all_gather(key_pages, "shard", axis=0, tiled=True)
    value_piece = lax.all_gather(value_pages, "shard", axis=0, tiled=True)
    page_count = key_piece.shape[0]
    page_len = key_piece.shape[1]
    step_pages = math.gcd(page_count, max(1, 512 // page_len))
    block_count = page_count // step_pages
    key_blocks = key_piece.reshape(block_count, step_pages * page_len, heads_here, DH)
    value_blocks = value_piece.reshape(block_count, step_pages * page_len, heads_here, DH)
    slot_blocks = page_slot.reshape(block_count, step_pages)

    def one_block(state, page_block):
        old_top, old_total, old_weighted = state
        key_block, value_block, slot_block = page_block
        owner = slot_block // PPG
        offset = (slot_block % PPG)[:, None] * page_len + jnp.arange(page_len, dtype=jnp.int32)[
            None, :
        ]
        is_valid = (owner[None, :, None] == request_group[:, None, None]) & (
            offset[None] < group_len[:, None, None]
        )
        is_valid = is_valid.reshape(req_count, step_pages * page_len)
        score = (
            jnp.einsum("rqhd,khd->rhqk", queries, key_block, preferred_element_type=jnp.float32)
            * score_scale
        )
        score = jnp.where(is_valid[:, None, None, :], score, -1e30)
        new_top = jnp.maximum(old_top, jnp.max(score, axis=-1))
        fade_factor = jnp.exp(old_top - new_top)
        weight = jnp.exp(score - new_top[..., None])
        new_total = old_total * fade_factor + jnp.sum(weight, axis=-1)
        new_weighted = old_weighted * fade_factor[..., None] + jnp.einsum(
            "rhqk,khd->rhqd",
            weight.astype(jnp.bfloat16),
            value_block,
            preferred_element_type=jnp.float32,
        )
        return ((new_top, new_total, new_weighted), None)

    running, _ = lax.scan(one_block, running, (key_blocks, value_blocks, slot_blocks))
    row_top, row_total, weighted = running
    context = (weighted / row_total[..., None]).astype(jnp.bfloat16)
    context = jnp.transpose(context, (0, 2, 1, 3)).reshape(req_count * query_len, head_width)

    def attn_terms(row_start, row_count):
        return jnp.dot(context, w_out, preferred_element_type=jnp.float32)

    first = combine_heads(attn_terms, token_rows, norm1_gain)
    inner = jnp.dot(first, w_inner, preferred_element_type=jnp.float32)
    active = jax.nn.gelu(inner, approximate=False).astype(jnp.bfloat16)

    def outer_terms(row_start, row_count):
        return jnp.dot(active, w_outer, preferred_element_type=jnp.float32)

    second = combine_heads(outer_terms, first, norm2_gain)
    projected = jnp.dot(second, w_project, preferred_element_type=jnp.float32)
    embed_rows = (
        projected * lax.rsqrt(jnp.sum(projected * projected, axis=-1, keepdims=True) + 1e-06)
    ).astype(jnp.bfloat16)
    embedded = embed_rows.reshape(req_count, query_len, embed_rows.shape[1])
    doc_each = doc_lengths.shape[1]
    holder = cand_ids // doc_each
    doc_tiles, tile_valid = build_tiles(doc_vectors, doc_lengths)
    maxima = doc_maxima(
        lax.all_gather(embed_rows, "shard", axis=0, tiled=True), doc_tiles, tile_valid
    )
    docs_here = tile_valid.shape[0]
    per_doc = jnp.sum(maxima.reshape(-1, query_len, docs_here), axis=1)
    is_mine = holder == lax.axis_index(("head", "shard"))
    local_doc = cand_ids % doc_each
    doc_hit = local_doc[..., None] == jnp.arange(docs_here, dtype=jnp.int32)
    contrib = jnp.sum(jnp.where(doc_hit, per_doc[:, None, :], 0.0), axis=-1)
    contrib = jnp.where(is_mine, contrib, 0.0)
    score_part = lax.psum_scatter(contrib, "shard", scatter_dimension=0, tiled=True)
    scores = lax.psum(score_part, "head")
    return (embedded, scores)


def solution(mesh):
    in_specs = (
        P("shard", None, None),
        P(None, "head"),
        P(None, "head"),
        P(None, "head"),
        P("head", None),
        P(),
        P(None, "head"),
        P("head", None),
        P(),
        P(),
        P("shard", None, "head"),
        P("shard", None, "head"),
        P(),
        P(),
        P("shard"),
        P(("head", "shard"), None),
        P(("head", "shard"), None),
        P("shard", None),
    )
    out_specs = (P("shard", None, None), P("shard", None))
    return jax.shard_map(
        per_device, mesh=mesh, in_specs=in_specs, out_specs=out_specs, check_vma=False
    )
```

profile of v0, /device:TPU:1, one launch (start us, length us, event | category | flops | bytes accessed | tf_op | source)
XLA Modules:
  0.0 1057.8 jit_solution(1644707749141062123)
XLA Ops:
  8.8 1.4 convolution_convert_fusion.4
  12.6 2.5 sort.17
  15.6 132.8 %all-gather.5.cloned.1.call-done = bf16[128,64,128]{2,1,0:T(8,128)(2,1)} async-done(((bf16[2,64,128]{2,1,0:T(8,128)(2,1)}), bf16[128,64,128]{2,1,0:T(8,128)(2,1)}) %all-gather.5.cloned.1.call-update) | async-done | bytes 2097168 | tf_op jit(solution)/shard_map/all_gather | solution.py:105
  148.4 8.2 reshape.284
  156.7 10.6 %copy.80 = bf16[16,512,2,64]{1,3,2,0:T(8,128)(2,1)} copy(bf16[16,512,2,64]{3,2,1,0:T(2,128)(2,1)} %reshape.284) | data formatting | bytes 4194304 | tf_op jit(solution)/shard_map/while | solution.py:143
  167.3 121.1 %all-gather.7.cloned.1.call-done = bf16[128,64,128]{2,1,0:T(8,128)(2,1)} async-done(((bf16[2,64,128]{2,1,0:T(8,128)(2,1)}), bf16[128,64,128]{2,1,0:T(8,128)(2,1)}) %all-gather.7.cloned.1.call-update) | async-done | bytes 2097168 | tf_op jit(solution)/shard_map/all_gather | solution.py:106
  288.4 8.2 reshape.285
  296.6 10.6 copy.82
  307.2 60.7 %while.27 = (s32[]{:T(128)}, f32[4,2,64]{2,0,1:T(4,128)S(1)}, f32[4,2,64]{2,0,1:T(4,128)S(1)}, f32[4,2,64,64]{2,3,0,1:T(8,128)S(1)}, s32[16,8]{1,0:T(8,128)S(1)}...) while((s32[]{:T(128)}, f32[4,2,64]{2,0,1:T(4,128)S(1)}, ...), condition=%wide.region_7.8_spmd, body=%wide.region_4.7_spmd.sunk | while | flops 70063840 | bytes 4855253 | solution.py:143
  313.3 1.4 fusion.154
  317.1 1.4 fusion.154
  328.5 1.4 fusion.154
  332.3 1.4 fusion.154
  339.9 1.4 fusion.154
  343.7 1.4 fusion.154
  347.5 1.4 fusion.154
  369.4 79.6 %all-reduce.4.cloned.1.call-done = bf16[256,1024]{1,0:T(8,128)(2,1)} async-done(((bf16[256,1024]{1,0:T(8,128)(2,1)}), bf16[256,1024]{1,0:T(8,128)(2,1)}) %all-reduce.4.cloned.1.call-update) | async-done | bytes 524304 | tf_op jit(solution)/shard_map/psum | solution.py:20
  451.9 2.7 convolution_convert_fusion
  454.8 75.4 %all-reduce.6.cloned.1.call-done = bf16[256,1024]{1,0:T(8,128)(2,1)} async-done(((bf16[256,1024]{1,0:T(8,128)(2,1)}), bf16[256,1024]{1,0:T(8,128)(2,1)}) %all-reduce.6.cloned.1.call-update) | async-done | bytes 524304 | tf_op jit(solution)/shard_map/psum | solution.py:20
  534.4 77.8 %all-gather = s32[64,4,16]{2,1,0:T(4,128)S(1)} all-gather(s32[1,4,16]{2,1,0:T(4,128)S(1)} %bitcast.140), channel_id=1, replica_groups=mesh['head'=8,'shard'=64] {'shard'}, dimensions={0}, use_global_device_ids=true | all-gather | bytes 16640 | tf_op jit(solution)/shard_map/all_gather | solution.py:99
  615.9 57.6 %all-gather.9.cloned.1.call-done = bf16[16384,128]{1,0:T(8,128)(2,1)} async-done(((bf16[256,128]{1,0:T(8,128)(2,1)}), bf16[16384,128]{1,0:T(8,128)(2,1)}) %all-gather.9.cloned.1.call-update) | async-done | bytes 4194320 | tf_op jit(solution)/shard_map/all_gather | solution.py:168
  673.5 79.8 %while.28 = (s32[]{:T(128)}, f32[64,256,4]{1,0,2:T(8,128)S(1)}, bf16[64,256,128]{2,1,0:T(8,128)(2,1)}, bf16[512,128]{1,0:T(8,128)(2,1)S(1)}, s32[4]{0:T(128)S(1)}, /*index=5*/s32[]{:T(128)}, s32[]{:T(128)}) while((s32[]{:T(128)}, f32[64,256,4]{1,0,2:T(8,128)S(1)}, bf16[64,256,128]{2,1,0:T(8,128)(2,1)}, ...), condition=%wide.region_18.19_spmd.clone, body=%wide.region_16.18_spmd.clone.sunk | while | flops 33816064 | bytes 218721 | solution.py:50
  753.7 220.8 %all-reduce = f32[256,16]{1,0:T(8,128)S(1)} all-reduce(f32[256,16]{1,0:T(8,128)S(1)} %copy.89), channel_id=2, replica_groups=mesh['head'=8,'shard'=64] {'shard'}, use_global_device_ids=true, to_apply=%region_21.22.clone | all-reduce | flops 4096 | bytes 32768
  974.6 76.7 %psum.23 = f32[4,16]{1,0:T(4,128)} all-reduce(f32[4,16]{1,0:T(4,128)S(1)} %constant_dynamic-slice_fusion.1), channel_id=1, replica_groups=mesh['head'=8,'shard'=64] {'head'}, use_global_device_ids=true, to_apply=%region_22.23 | all-reduce | flops 64 | bytes 512 | tf_op jit(solution)/shard_map/psum | solution.py:178
  (627 shorter events, 143.7 us)
Async XLA Ops:
  7.2 444.8 %copy-start = (bf16[512,1024]{1,0:T(8,128)(2,1)S(1)}, bf16[512,1024]{1,0:T(8,128)(2,1)}, u32[]{:S(2)}) copy-start(bf16[512,1024]{1,0:T(8,128)(2,1)} %param.29) | copy-start | bytes 3145732
  7.2 4.6 copy-start.1
  7.2 4.6 copy-start.5
  7.2 141.2 %all-gather.5.cloned.1.call-start = ((), (), s32[]{:S(2)}) async-start(), calls=%async_computation | async-start | bytes 2129920 | tf_op jit(solution)/shard_map/all_gather | solution.py:105
  7.9 280.4 %all-gather.7.cloned.1.call-start = ((), (), s32[]{:S(2)}) async-start(), calls=%async_computation.1 | async-start | bytes 2129920 | tf_op jit(solution)/shard_map/all_gather | solution.py:106
  8.7 440.3 %all-reduce.4.cloned.1.call-start = ((), (), s32[]{:S(2)}) async-start(), calls=%async_computation.2 | async-start | bytes 1048576 | tf_op jit(solution)/shard_map/psum | solution.py:20
  8.7 3.8 copy-start.12
  8.7 6.5 copy-start.13
  8.8 6.5 copy-start.14
  307.2 61.1 %copy-start.6 = (bf16[128,1024]{1,0:T(8,128)(2,1)S(1)}, bf16[128,1024]{1,0:T(8,128)(2,1)}, u32[]{:S(2)}) copy-start(bf16[128,1024]{1,0:T(8,128)(2,1)} %param.26) | copy-start | bytes 786436
  367.9 83.7 %copy-start.7 = (f32[1024]{0:T(1024)S(1)}, f32[1024]{0:T(1024)}, u32[]{:S(2)}) copy-start(f32[1024]{0:T(1024)} %param.27) | copy-start | bytes 12292
  369.3 82.6 %copy-start.9 = (bf16[1024,512]{1,0:T(8,128)(2,1)S(1)}, bf16[1024,512]{1,0:T(8,128)(2,1)}, u32[]{:S(2)}) copy-start(bf16[1024,512]{1,0:T(8,128)(2,1)} %param.28) | copy-start | bytes 3145732
  369.4 160.8 %all-reduce.6.cloned.1.call-start = ((), (), s32[]{:S(2)}) async-start(), calls=%async_computation.3 | async-start | bytes 1048576 | tf_op jit(solution)/shard_map/psum | solution.py:20
  449.0 2.7 copy-start.3
  454.7 78.2 %copy-start.10 = (bf16[1024,128]{1,0:T(8,128)(2,1)S(1)}, bf16[1024,128]{1,0:T(8,128)(2,1)}, u32[]{:S(2)}) copy-start(bf16[1024,128]{1,0:T(8,128)(2,1)} %param.31) | copy-start | bytes 786436
  454.7 78.2 %copy-start.11 = (f32[1024]{0:T(1024)S(1)}, f32[1024]{0:T(1024)}, u32[]{:S(2)}) copy-start(f32[1024]{0:T(1024)} %param.30) | copy-start | bytes 12292
  454.7 79.5 %copy-start.15 = (s32[1,4]{1,0:T(1,128)S(1)}, s32[1,4]{1,0:T(1,128)}, u32[]{:S(2)}) copy-start(s32[1,4]{1,0:T(1,128)} %param.38) | copy-start | bytes 52
  454.7 79.7 %copy-start.8 = (s32[4,16]{1,0:T(4,128)S(1)}, s32[4,16]{1,0:T(4,128)}, u32[]{:S(2)}) copy-start(s32[4,16]{1,0:T(4,128)} %param.39) | copy-start | bytes 772
  454.7 218.8 %all-gather.9.cloned.1.call-start = ((), (), s32[]{:S(2)}) async-start(), calls=%async_computation.4 | async-start | bytes 4259840 | tf_op jit(solution)/shard_map/all_gather | solution.py:168
  530.1 2.7 copy-start.4
  531.5 80.9 %copy-start.2 = (bf16[256,128]{1,0:T(8,128)(2,1)S(1)}, bf16[256,128]{1,0:T(8,128)(2,1)}, u32[]{:S(2)}) copy-start(bf16[256,128]{1,0:T(8,128)(2,1)} %param.37) | copy-start | bytes 196612
Sparse Core Ops, SparseCore 0:
  11.0 137.4 all-gather.4
  151.4 136.9 all-gather.6
  369.5 79.4 all-reduce.3
  454.8 75.2 all-reduce.5
  534.3 139.1 all-gather.8
where the time goes:
time: 1060 us
  waiting for transfers between devices  468 us (44%)
  blocking collectives  375 us (35%)
  matrix products  118 us (11%)
  local copies, waits for them, and re-layouts  51.2 us (5%)
  other arithmetic  26.6 us (3%)
  between operations  14.8 us (1%)
    unnamed x1, blocking collectives  221 us
    psum x2, waiting for transfers between devices, combine_heads(): lax.psum(term_rows(0, row_total).astype(jnp.bfloat16), 'head')  155 us
    all_gather x1, waiting for transfers between devices, per_device(): key_piece = lax.all_gather(key_pages, 'shard', axis=0, tiled=True)  133 us
    all_gather x1, waiting for transfers between devices, per_device(): value_piece = lax.all_gather(value_pages, 'shard', axis=0, tiled=True)  121 us
    all_gather x1, blocking collectives, per_device(): cand_ids = lax.all_gather(candidates, 'shard', axis=0, tiled=True)  77.8 us
    psum x1, blocking collectives, per_device(): scores = lax.psum(score_part, 'head')  76.7 us
    dot_general x64, matrix products, block_max(): jnp.einsum('ne,te->nt', block_rows, doc_tiles, preferred_element_type=jnp...  69.4 us
    all_gather x1, waiting for transfers between devices, per_device(): lax.all_gather(embed_rows, 'shard', axis=0, tiled=True)  57.6 us
  transfers between devices with their start and end apart: 5, of which 5 were waited for; matrix products, arithmetic and copies ran while one was open for 3% of the time, Pallas kernels for 0%

commit v1 on v0

--- a/solution.py
+++ b/solution.py
@@ -164,9 +164,10 @@
     doc_each = doc_lengths.shape[1]
     holder = cand_ids // doc_each
     doc_tiles, tile_valid = build_tiles(doc_vectors, doc_lengths)
-    maxima = doc_maxima(
-        lax.all_gather(embed_rows, "shard", axis=0, tiled=True), doc_tiles, tile_valid
-    )
+    lay_waves = lambda u: jnp.concatenate(
+        jax.lax.all_to_all(jnp.stack(jax.lax.axis_size("shard") * [u], 0), "shard", 0, 0), 0
+    )
+    maxima = doc_maxima(lay_waves(embed_rows), doc_tiles, tile_valid)
     docs_here = tile_valid.shape[0]
     per_doc = jnp.sum(maxima.reshape(-1, query_len, docs_here), axis=1)
     is_mine = holder == lax.axis_index(("head", "shard"))

time: 1060 us -> 1210 us (1.14)
  blocking collectives: 375 us -> 566 us
  waiting for transfers between devices: 468 us -> 410 us
  starting transfers between devices: 0.2 us -> 15.4 us
    all_gather x1, blocking collectives: 77.8 us -> 249 us  [per_device(): cand_ids = lax.all_gather(candidates, 'shard', axis=0, tiled=True)]
    all_gather x1 -> x0, waiting for transfers between devices: 57.6 us -> none  [per_device(): lax.all_gather(embed_rows, 'shard', axis=0, tiled=True)]
    psum x1, blocking collectives: 76.7 us -> 94.1 us  [per_device(): scores = lax.psum(score_part, 'head')]
    all_to_all x0 -> x1, starting transfers between devices: none -> 15.2 us  [per_device(): jax.lax.all_to_all(jnp.stack(jax.lax.axis_size('shard') * [u], 0), 'shard...]
  transfers between devices with their start and end apart: 5 -> 5, of which waited for: 5 -> 4; matrix products, arithmetic and copies ran while one was open for 3% -> 2% of each run, Pallas kernels for 0% -> 0%
where the time goes in v1:
time: 1210 us
  blocking collectives  566 us (47%)
  waiting for transfers between devices  410 us (34%)
  matrix products  118 us (10%)
  local copies, waits for them, and re-layouts  54.2 us (4%)
  other arithmetic  26 us (2%)
  starting transfers between devices  15.4 us (1%)
  between operations  14.8 us (1%)
    all_gather x1, blocking collectives, per_device(): cand_ids = lax.all_gather(candidates, 'shard', axis=0, tiled=True)  249 us
    unnamed x1, blocking collectives  222 us
    psum x2, waiting for transfers between devices, combine_heads(): lax.psum(term_rows(0, row_total).astype(jnp.bfloat16), 'head')  155 us
    all_gather x1, waiting for transfers between devices, per_device(): key_piece = lax.all_gather(key_pages, 'shard', axis=0, tiled=True)  133 us
    all_gather x1, waiting for transfers between devices, per_device(): value_piece = lax.all_gather(value_pages, 'shard', axis=0, tiled=True)  121 us
    psum x1, blocking collectives, per_device(): scores = lax.psum(score_part, 'head')  94.1 us
    dot_general x64, matrix products, block_max(): jnp.einsum('ne,te->nt', block_rows, doc_tiles, preferred_element_type=jnp...  69.4 us
  transfers between devices with their start and end apart: 5, of which 4 were waited for; matrix products, arithmetic and copies ran while one was open for 2% of the time, Pallas kernels for 0%

profile of v1, /device:TPU:1, one launch (start us, length us, event | category | flops | bytes accessed | tf_op | source)
XLA Modules:
  0.0 1207.9 jit_solution(15664598387911425527)
XLA Ops:
  8.8 1.4 convolution_convert_fusion.4
  12.6 2.5 sort.17
  15.6 132.8 %all-gather.4.cloned.1.call-done = bf16[128,64,128]{2,1,0:T(8,128)(2,1)} async-done(((bf16[2,64,128]{2,1,0:T(8,128)(2,1)}), bf16[128,64,128]{2,1,0:T(8,128)(2,1)}) %all-gather.4.cloned.1.call-update) | async-done | bytes 2097168 | tf_op jit(solution)/shard_map/all_gather | solution.py:105
  148.4 8.2 reshape.282
  156.7 10.6 copy.80
  167.3 121.1 %all-gather.6.cloned.1.call-done = bf16[128,64,128]{2,1,0:T(8,128)(2,1)} async-done(((bf16[2,64,128]{2,1,0:T(8,128)(2,1)}), bf16[128,64,128]{2,1,0:T(8,128)(2,1)}) %all-gather.6.cloned.1.call-update) | async-done | bytes 2097168 | tf_op jit(solution)/shard_map/all_gather | solution.py:106
  288.4 8.2 reshape.283
  296.6 10.6 copy.82
  307.2 60.7 %while.27 = (s32[]{:T(128)}, f32[4,2,64]{2,0,1:T(4,128)S(1)}, f32[4,2,64]{2,0,1:T(4,128)S(1)}, f32[4,2,64,64]{2,3,0,1:T(8,128)S(1)}, s32[16,8]{1,0:T(8,128)S(1)}...) while((s32[]{:T(128)}, f32[4,2,64]{2,0,1:T(4,128)S(1)}, ...), condition=%wide.region_7.8_spmd, body=%wide.region_4.7_spmd.sunk | while | flops 70063840 | bytes 4855253 | solution.py:143
  313.3 1.4 fusion.154
  317.1 1.4 fusion.154
  328.5 1.4 fusion.154
  332.3 1.4 fusion.154
  339.9 1.4 fusion.154
  343.7 1.4 fusion.154
  369.4 79.6 %all-reduce.4.cloned.1.call-done = bf16[256,1024]{1,0:T(8,128)(2,1)} async-done(((bf16[256,1024]{1,0:T(8,128)(2,1)}), bf16[256,1024]{1,0:T(8,128)(2,1)}) %all-reduce.4.cloned.1.call-update) | async-done | bytes 524304 | tf_op jit(solution)/shard_map/psum | solution.py:20
  451.9 2.7 convolution_convert_fusion
  454.7 75.5 %all-reduce.6.cloned.1.call-done = bf16[256,1024]{1,0:T(8,128)(2,1)} async-done(((bf16[256,1024]{1,0:T(8,128)(2,1)}), bf16[256,1024]{1,0:T(8,128)(2,1)}) %all-reduce.6.cloned.1.call-update) | async-done | bytes 524304 | tf_op jit(solution)/shard_map/psum | solution.py:20
  533.5 3.0 stack.2
  536.5 15.2 %all-to-all-start = ((bf16[64,256,128]{2,1,0:T(8,128)(2,1)}), bf16[64,256,128]{2,1,0:T(8,128)(2,1)}, u32[]{:S(2)}, u32[]{:S(2)}) async-start(bf16[64,256,128]{2,1,0:T(8,128)(2,1)} %stack.2), calls=%async_computation | async-start | bytes 8388608 | tf_op jit(solution)/shard_map/all_to_all | solution.py:168
  551.9 249.5 %all-gather = s32[64,4,16]{2,1,0:T(4,128)S(1)} all-gather(s32[1,4,16]{2,1,0:T(4,128)S(1)} %bitcast.139), channel_id=1, replica_groups=mesh['head'=8,'shard'=64] {'shard'}, dimensions={0}, use_global_device_ids=true | all-gather | bytes 16640 | tf_op jit(solution)/shard_map/all_gather | solution.py:99
  805.0 79.8 %while.28 = (s32[]{:T(128)}, f32[64,256,4]{1,0,2:T(8,128)S(1)}, bf16[64,256,128]{2,1,0:T(8,128)(2,1)}, bf16[512,128]{1,0:T(8,128)(2,1)S(1)}, s32[4]{0:T(128)S(1)}, /*index=5*/s32[]{:T(128)}, s32[]{:T(128)}) while((s32[]{:T(128)}, f32[64,256,4]{1,0,2:T(8,128)S(1)}, bf16[64,256,128]{2,1,0:T(8,128)(2,1)}, ...), condition=%wide.region_18.19_spmd.clone, body=%wide.region_16.18_spmd.clone.sunk | while | flops 33816064 | bytes 218721 | solution.py:50
  885.2 222.0 %all-reduce = f32[256,16]{1,0:T(8,128)S(1)} all-reduce(f32[256,16]{1,0:T(8,128)S(1)} %copy.89), channel_id=2, replica_groups=mesh['head'=8,'shard'=64] {'shard'}, use_global_device_ids=true, to_apply=%region_21.22.clone | all-reduce | flops 4096 | bytes 32768
  1107.2 94.1 %psum.23 = f32[4,16]{1,0:T(4,128)} all-reduce(f32[4,16]{1,0:T(4,128)S(1)} %constant_dynamic-slice_fusion.1), channel_id=1, replica_groups=mesh['head'=8,'shard'=64] {'head'}, use_global_device_ids=true, to_apply=%region_22.23 | all-reduce | flops 64 | bytes 512 | tf_op jit(solution)/shard_map/psum | solution.py:179
  (629 shorter events, 144.4 us)
Async XLA Ops:
  7.2 444.8 %copy-start = (bf16[512,1024]{1,0:T(8,128)(2,1)S(1)}, bf16[512,1024]{1,0:T(8,128)(2,1)}, u32[]{:S(2)}) copy-start(bf16[512,1024]{1,0:T(8,128)(2,1)} %param.29) | copy-start | bytes 3145732
  7.2 4.6 copy-start.1
  7.2 4.6 copy-start.6
  7.2 141.2 %all-gather.4.cloned.1.call-start = ((), (), s32[]{:S(2)}) async-start(), calls=%async_computation.1 | async-start | bytes 2129920 | tf_op jit(solution)/shard_map/all_gather | solution.py:105
  7.9 280.4 %all-gather.6.cloned.1.call-start = ((), (), s32[]{:S(2)}) async-start(), calls=%async_computation.2 | async-start | bytes 2129920 | tf_op jit(solution)/shard_map/all_gather | solution.py:106
  8.7 440.3 %all-reduce.4.cloned.1.call-start = ((), (), s32[]{:S(2)}) async-start(), calls=%async_computation.3 | async-start | bytes 1048576 | tf_op jit(solution)/shard_map/psum | solution.py:20
  8.7 3.8 copy-start.13
  8.7 6.5 copy-start.14
  8.8 6.5 copy-start.15
  307.2 61.1 %copy-start.7 = (bf16[128,1024]{1,0:T(8,128)(2,1)S(1)}, bf16[128,1024]{1,0:T(8,128)(2,1)}, u32[]{:S(2)}) copy-start(bf16[128,1024]{1,0:T(8,128)(2,1)} %param.26) | copy-start | bytes 786436
  367.9 83.7 %copy-start.8 = (f32[1024]{0:T(1024)S(1)}, f32[1024]{0:T(1024)}, u32[]{:S(2)}) copy-start(f32[1024]{0:T(1024)} %param.27) | copy-start | bytes 12292
  369.3 82.6 %copy-start.10 = (bf16[1024,512]{1,0:T(8,128)(2,1)S(1)}, bf16[1024,512]{1,0:T(8,128)(2,1)}, u32[]{:S(2)}) copy-start(bf16[1024,512]{1,0:T(8,128)(2,1)} %param.28) | copy-start | bytes 3145732
  369.4 160.8 %all-reduce.6.cloned.1.call-start = ((), (), s32[]{:S(2)}) async-start(), calls=%async_computation.4 | async-start | bytes 1048576 | tf_op jit(solution)/shard_map/psum | solution.py:20
  449.0 2.7 copy-start.3
  454.7 78.2 %copy-start.11 = (bf16[1024,128]{1,0:T(8,128)(2,1)S(1)}, bf16[1024,128]{1,0:T(8,128)(2,1)}, u32[]{:S(2)}) copy-start(bf16[1024,128]{1,0:T(8,128)(2,1)} %param.31) | copy-start | bytes 786436
  454.7 78.2 %copy-start.12 = (f32[1024]{0:T(1024)S(1)}, f32[1024]{0:T(1024)}, u32[]{:S(2)}) copy-start(f32[1024]{0:T(1024)} %param.30) | copy-start | bytes 12292
  530.1 2.7 copy-start.4
  533.5 3.0 copy-start.5
  536.5 15.3 %copy-start.16 = (s32[1,4]{1,0:T(1,128)S(1)}, s32[1,4]{1,0:T(1,128)}, u32[]{:S(2)}) copy-start(s32[1,4]{1,0:T(1,128)} %param.38) | copy-start | bytes 52
  536.5 15.4 %copy-start.9 = (s32[4,16]{1,0:T(4,128)S(1)}, s32[4,16]{1,0:T(4,128)}, u32[]{:S(2)}) copy-start(s32[4,16]{1,0:T(4,128)} %param.39) | copy-start | bytes 772
  536.5 265.1 %copy-start.2 = (bf16[256,128]{1,0:T(8,128)(2,1)S(1)}, bf16[256,128]{1,0:T(8,128)(2,1)}, u32[]{:S(2)}) copy-start(bf16[256,128]{1,0:T(8,128)(2,1)} %param.37) | copy-start | bytes 196612
  536.5 268.5 %all-to-all-start = ((bf16[64,256,128]{2,1,0:T(8,128)(2,1)}), bf16[64,256,128]{2,1,0:T(8,128)(2,1)}, u32[]{:S(2)}, u32[]{:S(2)}) async-start(bf16[64,256,128]{2,1,0:T(8,128)(2,1)} %stack.2), calls=%async_computation | async-start | bytes 8388608 | tf_op jit(solution)/shard_map/all_to_all | solution.py:168
Sparse Core Ops, SparseCore 0:
  11.0 137.4 all-gather.3
  151.4 136.9 all-gather.5
  369.5 79.4 all-reduce.3
  454.8 75.2 all-reduce.5
